TPU v7x, 512 devices: a whole 4x4x16 slice. The times are simulated.
512 devices in a mesh: row: 16 (over x, y), col: 32 (over z, core).
Axes of the slice: x: 4, y: 4, z: 16, core: 2. Of those that a mesh axis runs over, the one named last changes fastest.
Arguments:
- inputs: bfloat16 [768, 6144], P('col', 'row'), may hold values from -6 to 6
- weight: bfloat16 [6144, 24576], P('row', 'col'), may hold values from -0.078125 to 0.078125
- cotangent: bfloat16 [768, 24576], P('row', 'col'), may hold values from -6 to 6
Outputs:
- input_grad: bfloat16 [768, 6144], P('col', 'row')
- weight_grad: float32 [6144, 24576], P('row', 'col')
All inputs are finite; a program needn't handle non-finite values.
Results may differ from a plain program's by a relative error of at most 0.0049.
Values may be sent and summed in bfloat16 or wider, within the bound.
A program may use at most 64 MiB of HBM per device.

v0:
```python
import jax
import jax.numpy as jnp
from jax import lax
from jax.sharding import PartitionSpec as P


def gelu_slope(preact):
    return (
        0.5 * (1.0 + jax.scipy.special.erf(preact * 0.7071067811865476))
        + preact * jnp.exp(-0.5 * preact * preact) * 0.3989422804014327
    )


def shards(inputs, weight, cotangent):
    gathered = lax.all_gather(inputs, "col", axis=0, tiled=True)
    rows_here = gathered
    preact = lax.psum_scatter(
        jnp.dot(rows_here, weight, preferred_element_type=jnp.float32),
        "row",
        scatter_dimension=0,
        tiled=True,
    )
    grad_share = (cotangent.astype(jnp.float32) * gelu_slope(preact)).astype(jnp.bfloat16)
    grad_hidden = lax.all_gather(grad_share, "row", axis=0, tiled=True)
    rows_here = grad_hidden
    input_grad = lax.psum_scatter(
        lax.dot_general(
            rows_here, weight, (((1,), (1,)), ((), ())), preferred_element_type=jnp.float32
        ),
        "col",
        scatter_dimension=0,
        tiled=True,
    ).astype(jnp.bfloat16)
    weight_grad = lax.dot_general(
        gathered, grad_hidden, (((0,), (0,)), ((), ())), preferred_element_type=jnp.float32
    )
    return (input_grad, weight_grad)


def solution(mesh):
    placed = (P("col", "row"), P("row", "col"), P("row", "col"))
    return jax.shard_map(
        shards,
        mesh=mesh,
        in_specs=placed,
        out_specs=(P("col", "row"), P("row", "col")),
        check_vma=False,
    )
```

profile of v0, /device:TPU:6, one launch (start us, length us, event | category | flops | bytes accessed | tf_op | source)
XLA Modules:
  0.0 314.4 jit_solution(44614728491709948)
XLA Ops:
  7.2 0.0 copy-start
  7.2 0.0 reduce-scatter.5.cloned.1.call-start
  7.2 38.2 %all_gather.6 = bf16[768,384]{1,0:T(8,128)(2,1)S(1)} all-gather(bf16[24,384]{1,0:T(8,128)(2,1)} %param.3), channel_id=1, replica_groups=mesh['row'=16,'col'=32] {'col'}, dimensions={0}, use_global_device_ids=true | all-gather | bytes 608256 | tf_op jit(solution)/shard_map/all_gather | solution.py:15
  45.5 0.0 copy-done
  45.5 2.2 fusion.6
  47.6 0.0 copy-start.2
  47.6 0.0 reduce-scatter.5.cloned.1.call-update
  47.7 0.0 all-gather.2.cloned.1.call-start
  47.7 85.9 %reduce-scatter.5.cloned.1.call-done = f32[48,768]{1,0:T(8,128)} async-done(((f32[768,768]{1,0:T(8,128)}), f32[48,768]{1,0:T(8,128)}) %reduce-scatter.5.cloned.1.call-update) | async-done | bytes 147472 | tf_op jit(solution)/shard_map/reduce_scatter | solution.py:17
  133.6 0.0 copy-done.2
  133.6 1.6 fusion.5
  135.2 0.0 all-gather.2.cloned.1.call-update
  135.2 0.0 reduce-scatter.7.cloned.1.call-start
  135.3 59.8 %all-gather.2.cloned.1.call-done = bf16[768,768]{1,0:T(8,128)(2,1)} async-done(((bf16[48,768]{1,0:T(8,128)(2,1)}), bf16[768,768]{1,0:T(8,128)(2,1)}) %all-gather.2.cloned.1.call-update) | async-done | bytes 1179664 | tf_op jit(solution)/shard_map/all_gather | solution.py:24
  195.0 3.1 fusion.7
  198.1 0.0 copy-start.1
  198.1 0.0 reduce-scatter.7.cloned.1.call-update
  198.2 1.2 copy-done.1
  199.4 0.8 convolution_bitcast_fusion
  200.2 1.4 copy.6
  201.6 104.9 %reduce-scatter.7.cloned.1.call-done = f32[24,384]{1,0:T(8,128)} async-done(((f32[768,384]{1,0:T(8,128)}), f32[24,384]{1,0:T(8,128)}) %reduce-scatter.7.cloned.1.call-update) | async-done | bytes 36880
  306.5 1.4 convert_element_type.11
Async XLA Ops:
  7.2 38.3 %copy-start = (bf16[384,768]{1,0:T(8,128)(2,1)S(1)}, bf16[384,768]{1,0:T(8,128)(2,1)}, u32[]{:S(2)}) copy-start(bf16[384,768]{1,0:T(8,128)(2,1)} %param.4) | copy-start | bytes 1769476
  7.2 126.4 %reduce-scatter.5.cloned.1.call-start = ((), (), s32[]{:S(2)}) async-start(), calls=%async_computation.2 | async-start | bytes 2506752 | tf_op jit(solution)/shard_map/reduce_scatter | solution.py:17
  47.6 85.9 %copy-start.2 = (bf16[48,768]{1,0:T(8,128)(2,1)S(1)}, bf16[48,768]{1,0:T(8,128)(2,1)}, u32[]{:S(2)}) copy-start(bf16[48,768]{1,0:T(8,128)(2,1)} %param.5) | copy-start | bytes 221188
  47.7 147.4 %all-gather.2.cloned.1.call-start = ((), (), s32[]{:S(2)}) async-start(), calls=%async_computation.3 | async-start | bytes 1253376 | tf_op jit(solution)/shard_map/all_gather | solution.py:24
  135.2 171.3 %reduce-scatter.7.cloned.1.call-start = ((), (), s32[]{:S(2)}) async-start(), calls=%async_computation.4 | async-start | bytes 1216512
  198.1 1.3 copy-start.1
Sparse Core Ops, SparseCore 0:
  47.8 85.7 reduce-scatter.4
  137.2 57.7 all-gather.1
  198.3 108.1 reduce-scatter.6
where the time goes:
time: 315 us; the launch traced here: 314 us
  waiting for transfers between devices  251 us (80%)
  blocking collectives  38.2 us (12%)
  between operations  13.8 us (4%)
  matrix products  6.05 us (2%)
    unnamed x4, waiting for transfers between devices  105 us
    reduce_scatter x1, waiting for transfers between devices, shards(): lax.psum_scatter(jnp.dot(rows_here, weight, preferred_element_type=jnp.fl...  85.9 us
    all_gather x1, waiting for transfers between devices, shards(): grad_hidden = lax.all_gather(grad_share, 'row', axis=0, tiled=True)  59.8 us
    all_gather x1, blocking collectives, shards(): gathered = lax.all_gather(inputs, 'col', axis=0, tiled=True)  38.2 us
  transfers between devices with their start and end apart: 3, of which 3 were waited for; matrix products, arithmetic and copies ran while one was open for 1% of the time, Pallas kernels for 0%

commit v1 on v0

v1 whole, which is shorter than its diff:
```python
import functools
import math

import jax
import jax.numpy as jnp
from jax import lax
from jax.experimental import pallas as pl
from jax.experimental.pallas import tpu as pltpu
from jax.sharding import PartitionSpec as P

MESH = pl.DeviceIdType.MESH
F32 = jnp.float32
BF16 = jnp.bfloat16


def gelu_slope(preact):
    return (
        0.5 * (1.0 + lax.erf(preact * 0.7071067811865476))
        + preact * jnp.exp(-0.5 * preact * preact) * 0.3989422804014327
    )


def kernel(
    rows,
    cols,
    x_ref,
    w_ref,
    ct_ref,
    ig_ref,
    wg_ref,
    gat,
    part,
    pin,
    gh,
    full,
    give,
    take,
    pair,
    landed,
    acc,
    zs,
    zr,
    fs,
    fr,
    ps,
    pr,
    gs,
    gr,
    es,
    er,
    qs,
    qr,
):
    ny = math.isqrt(rows)
    nx = rows // ny
    nz = cols // 2
    r = lax.axis_index("row")
    c = lax.axis_index("col")
    z = c // 2
    core = c % 2
    other = 2 * z + 1 - core
    x0 = r // ny
    y0 = r % ny
    share = x_ref.shape[0]
    width = x_ref.shape[1]
    hidden = w_ref.shape[1]
    toks = ct_ref.shape[0]

    def z_peer(d):
        return 2 * ((z + d) % nz) + core

    def near(k):
        half = (k + 1) // 2
        odd = k % 2
        return odd * half + (1 - odd) * (nz - half)

    def row_at(k):
        return ((x0 + k // ny) % nx) * ny + (y0 + k % ny) % ny

    def row_from(k):
        return ((x0 + nx - k // ny) % nx) * ny + (y0 + ny - k % ny) % ny

    def to(src, dst, send, recv, row, col):
        return pltpu.make_async_remote_copy(
            src_ref=src,
            dst_ref=dst,
            send_sem=send,
            recv_sem=recv,
            device_id=(row, col),
            device_id_type=MESH,
        )

    barrier = pltpu.get_barrier_semaphore()

    @pl.loop(1, nz)
    def _(k):
        pl.semaphore_signal(barrier, inc=1, device_id=(r, z_peer(near(k))), device_id_type=MESH)

    @pl.loop(1, rows)
    def _(k):
        pl.semaphore_signal(barrier, inc=1, device_id=(row_at(k), c), device_id_type=MESH)

    pl.semaphore_signal(barrier, inc=1, device_id=(r, other), device_id_type=MESH)
    pl.semaphore_wait(barrier, nz - 1 + rows - 1 + 1)

    @pl.loop(1, nz)
    def _(k):
        d = near(k)
        to(x_ref, gat.at[c], zs.at[d], zr.at[d], r, z_peer(d)).start()

    to(x_ref, gat.at[c], fs.at[0], fr.at[0], r, other).start()
    gat[pl.ds(c, 1)] = x_ref[...].reshape(1, share, width)

    @pl.loop(1, nz)
    def _(k):
        d = near(k)
        from_col = 2 * ((z + nz - d) % nz) + core
        to(x_ref, gat.at[from_col], zs.at[d], zr.at[d], r, c).wait_recv()
        to(gat.at[from_col], gat.at[from_col], fs.at[d], fr.at[d], r, other).start()

    @pl.loop(0, nz)
    def _(k):
        from_col = 2 * ((z + nz - k) % nz) + 1 - core
        to(x_ref, gat.at[from_col], fs.at[k], fr.at[k], r, other).wait_recv()

    for g in range(nx):
        xg = (x0 + g) % nx
        lhs = gat[pl.ds(2 * ny * xg, 2 * ny)].reshape(ny * toks, width)
        block = jnp.dot(lhs, w_ref[...], preferred_element_type=F32)
        if g == 0:
            full[...] = block.reshape(ny, toks, hidden)
            acc[...] = full[pl.ds(y0, 1)].reshape(toks, hidden)
        part[pl.ds(ny * xg, ny)] = block.astype(BF16).reshape(ny, toks, hidden)

        @pl.loop(1 if g == 0 else 0, ny)
        def _(j):
            k = g * ny + j
            peer = row_at(k)
            to(part.at[peer], pin.at[k], ps.at[k], pr.at[k], peer, c).start()

    @pl.loop(1, rows)
    def _(k):
        to(part.at[k], pin.at[k], ps.at[k], pr.at[k], r, other).wait_recv()
        acc[...] += pin[pl.ds(k, 1)].reshape(toks, hidden).astype(F32)

    gh[pl.ds(r, 1)] = (
        (ct_ref[...].astype(F32) * gelu_slope(acc[...])).astype(BF16).reshape(1, toks, hidden)
    )

    @pl.loop(1, rows)
    def _(k):
        to(gh.at[r], gh.at[r], gs.at[k], gr.at[k], row_at(k), c).start()

    for g in range(nx):
        xg = (x0 + nx - g) % nx

        @pl.loop(1 if g == 0 else 0, ny)
        def _(j):
            k = g * ny + j
            to(gh.at[r], gh.at[row_from(k)], gs.at[k], gr.at[k], r, other).wait_recv()

        lhs = gh[pl.ds(ny * xg, ny)].reshape(ny * toks, hidden)
        block = lax.dot_general(
            lhs, w_ref[...], (((1,), (1,)), ((), ())), preferred_element_type=F32
        )
        pair[pl.ds(2 * ny * xg, 2 * ny)] = block.reshape(2 * ny, share, width)
        for j in range(ny):
            at = ny * xg + j
            give[pl.ds(at, 1)] = pair[pl.ds(2 * at + 1 - core, 1)].astype(BF16)
        groups = pl.ds(ny * xg, ny)
        to(give.at[groups], take.at[groups], es.at[g], er.at[g], r, other).start()

    for g in range(nx):
        xg = (x0 + nx - g) % nx
        groups = pl.ds(ny * xg, ny)
        to(give.at[groups], take.at[groups], es.at[g], er.at[g], r, other).wait()

    for k in range(nz):
        at = (z + k) % nz
        mine = pair[pl.ds(2 * at + core, 1)] + take[pl.ds(at, 1)].astype(F32)
        if k == 0:
            pair[pl.ds(c, 1)] = mine
        else:
            give[pl.ds(at, 1)] = mine.astype(BF16)
            to(give.at[at], landed.at[k], qs.at[k], qr.at[k], r, z_peer(k)).start()

    wg_ref[...] = lax.dot_general(
        gat[...].reshape(rows * toks, width),
        gh[...].reshape(rows * toks, hidden),
        (((0,), (0,)), ((), ())),
        preferred_element_type=F32,
    )

    total = pair[pl.ds(c, 1)].reshape(share, width)
    for k in range(1, nz):
        to(give.at[k], landed.at[k], qs.at[k], qr.at[k], r, other).wait_recv()
        total = total + landed[k].astype(F32)
    ig_ref[...] = total.astype(BF16)

    to(x_ref, gat.at[c], fs.at[0], fr.at[0], r, other).wait_send()

    @pl.loop(1, nz)
    def _(k):
        to(x_ref, gat.at[c], zs.at[k], zr.at[k], r, other).wait_send()
        to(x_ref, gat.at[c], fs.at[k], fr.at[k], r, other).wait_send()
        to(give.at[0], landed.at[k], qs.at[k], qr.at[k], r, other).wait_send()

    @pl.loop(1, rows)
    def _(k):
        to(part.at[k], pin.at[k], ps.at[k], pr.at[k], r, other).wait_send()
        to(gh.at[r], gh.at[r], gs.at[k], gr.at[k], r, other).wait_send()


def shards(rows, cols, inputs, weight, cotangent):
    share, width = inputs.shape
    hidden = weight.shape[1]
    toks = cotangent.shape[0]
    nz = cols // 2
    ny = math.isqrt(rows)
    dma = pltpu.SemaphoreType.DMA
    return pl.pallas_call(
        functools.partial(kernel, rows, cols),
        out_shape=(
            jax.ShapeDtypeStruct((share, width), BF16),
            jax.ShapeDtypeStruct((width, hidden), F32),
        ),
        in_specs=[pl.BlockSpec(memory_space=pltpu.VMEM)] * 3,
        out_specs=(pl.BlockSpec(memory_space=pltpu.VMEM),) * 2,
        scratch_shapes=[
            pltpu.VMEM((cols, share, width), BF16),
            pltpu.VMEM((rows, toks, hidden), BF16),
            pltpu.VMEM((rows, toks, hidden), BF16),
            pltpu.VMEM((rows, toks, hidden), BF16),
            pltpu.VMEM((ny, toks, hidden), F32),
            pltpu.VMEM((nz, share, width), BF16),
            pltpu.VMEM((nz, share, width), BF16),
            pltpu.VMEM((cols, share, width), F32),
            pltpu.VMEM((nz, share, width), BF16),
            pltpu.VMEM((toks, hidden), F32),
            dma((nz,)),
            dma((nz,)),
            dma((nz,)),
            dma((nz,)),
            dma((rows,)),
            dma((rows,)),
            dma((rows,)),
            dma((rows,)),
            dma((ny,)),
            dma((ny,)),
            dma((nz,)),
            dma((nz,)),
        ],
        compiler_params=pltpu.CompilerParams(
            collective_id=0, has_side_effects=True, vmem_limit_bytes=56 * 1024 * 1024
        ),
    )(inputs, weight, cotangent)


def solution(mesh):
    rows, cols = mesh.shape["row"], mesh.shape["col"]
    placed = (P("col", "row"), P("row", "col"), P("row", "col"))
    return jax.shard_map(
        functools.partial(shards, rows, cols),
        mesh=mesh,
        in_specs=placed,
        out_specs=(P("col", "row"), P("row", "col")),
        check_vma=False,
    )
```

time: 315 us -> 98.8 us (0.31)
  the two profiles are of different devices: /device:TPU:6 before, /device:TPU:1 now
where the time goes in v1:
time: 98.8 us; the launch traced here: 98.6 us
  Pallas kernels  94.2 us (95%)
  local copies, waits for them, and re-layouts  3.69 us (4%)
    pallas_call x1, Pallas kernels, shards(): pl.pallas_call(functools.partial(kernel, rows, cols), out_shape=(jax.Shap...  94.2 us
    unnamed x2, local copies, waits for them, and re-layouts  3.69 us

profile of v1, /device:TPU:1, one launch (start us, length us, event | category | flops | bytes accessed | tf_op | source)
XLA Modules:
  0.0 98.6 jit_solution(16749518424215808272)
XLA Ops:
  0.6 94.2 %shard_map.50 = (bf16[24,384]{1,0:T(8,128)(2,1)}, f32[384,768]{1,0:T(8,128)}) custom-call(bf16[24,384]{1,0:T(8,128)(2,1)} %x_ref.1, bf16[384,768]{1,0:T(8,128)(2,1)} %w_ref.1, bf16[48,768]{1,0:T(8,128)(2,1)} %ct_ref.1), custom_call_target="tpu_custom_call" | custom-call | tf_op jit(solution)/shard_map/pallas_call | solution.py:221
  94.9 1.3 %copy.7 = bf16[24,384]{1,0:T(8,128)(2,1)} copy(bf16[24,384]{1,0:T(8,128)(2,1)} %get-tuple-element.4) | data formatting | bytes 36864
  96.2 2.4 %copy.8 = f32[384,768]{1,0:T(8,128)} copy(f32[384,768]{1,0:T(8,128)} %get-tuple-element.5) | data formatting | bytes 2359296

commit v2 on v1

--- a/solution.py
+++ b/solution.py
@@ -36,7 +36,10 @@
     give,
     take,
     pair,
-    landed,
+    near_out,
+    near_in,
+    far_out,
+    far_in,
     acc,
     zs,
     zr,
@@ -50,6 +53,8 @@
     er,
     qs,
     qr,
+    us,
+    ur,
 ):
     ny = math.isqrt(rows)
     nx = rows // ny
@@ -66,13 +71,8 @@
     hidden = w_ref.shape[1]
     toks = ct_ref.shape[0]
 
-    def z_peer(d):
-        return 2 * ((z + d) % nz) + core
-
-    def near(k):
-        half = (k + 1) // 2
-        odd = k % 2
-        return odd * half + (1 - odd) * (nz - half)
+    def chip(d):
+        return (z + d + 2 * nz) % nz
 
     def row_at(k):
         return ((x0 + k // ny) % nx) * ny + (y0 + k % ny) % ny
@@ -92,36 +92,66 @@
 
     barrier = pltpu.get_barrier_semaphore()
 
-    @pl.loop(1, nz)
-    def _(k):
-        pl.semaphore_signal(barrier, inc=1, device_id=(r, z_peer(near(k))), device_id_type=MESH)
+    for d in (-4, 4, -2, 2, -1, 1):
+        pl.semaphore_signal(
+            barrier, inc=1, device_id=(r, 2 * chip(d) + core), device_id_type=MESH
+        )
 
     @pl.loop(1, rows)
     def _(k):
         pl.semaphore_signal(barrier, inc=1, device_id=(row_at(k), c), device_id_type=MESH)
 
     pl.semaphore_signal(barrier, inc=1, device_id=(r, other), device_id_type=MESH)
-    pl.semaphore_wait(barrier, nz - 1 + rows - 1 + 1)
-
-    @pl.loop(1, nz)
-    def _(k):
-        d = near(k)
-        to(x_ref, gat.at[c], zs.at[d], zr.at[d], r, z_peer(d)).start()
-
-    to(x_ref, gat.at[c], fs.at[0], fr.at[0], r, other).start()
+    pl.semaphore_wait(barrier, 6 + rows - 1 + 1)
+
+    turn = 1 - 2 * core
+    messages = [(-4, 0), (4, 0), (-4 * turn, 4 * turn)]
+    messages += [(-1, of) for of in (0, 4, -4, 8)] + [(1, of) for of in (0, 4, -4, 8)]
+    messages += [(-2, 0), (-2, 4), (2, 0), (2, -4)]
+
+    def gather_send(*numbers):
+        for m in numbers:
+            hop, of = messages[m]
+            slot = 2 * chip(of) + core
+            src = x_ref if type(of) is int and of == 0 else gat.at[slot]
+            to(src, gat.at[slot], zs.at[m], zr.at[m], r, 2 * chip(hop) + core).start()
+
+    def gather_wait(*numbers):
+        for m in numbers:
+            hop, of = messages[m]
+            slot = 2 * chip(of - hop) + core
+            to(x_ref, gat.at[slot], zs.at[m], zr.at[m], r, other).wait_recv()
+
+    def forward(*numbers):
+        for m in numbers:
+            hop, of = messages[m]
+            slot = 2 * chip(of - hop) + core
+            to(gat.at[slot], gat.at[slot], fs.at[m], fr.at[m], r, other).start()
+
+    last = len(messages)
+    gather_send(0, 1, 3, 7, 11, 13)
+    to(x_ref, gat.at[c], fs.at[last], fr.at[last], r, other).start()
     gat[pl.ds(c, 1)] = x_ref[...].reshape(1, share, width)
-
-    @pl.loop(1, nz)
-    def _(k):
-        d = near(k)
-        from_col = 2 * ((z + nz - d) % nz) + core
-        to(x_ref, gat.at[from_col], zs.at[d], zr.at[d], r, c).wait_recv()
-        to(gat.at[from_col], gat.at[from_col], fs.at[d], fr.at[d], r, other).start()
+    gather_wait(3, 7)
+    forward(3, 7)
+    gather_wait(11, 13)
+    forward(11, 13)
+    gather_wait(0, 1)
+    gather_send(2, 4, 8, 5, 9, 12, 14)
+    forward(0, 1)
+    gather_wait(4, 5, 8, 9)
+    forward(4, 5, 8, 9)
+    gather_wait(2)
+    gather_send(6, 10)
+    forward(2)
+    gather_wait(12, 14)
+    forward(12, 14)
+    gather_wait(6, 10)
+    forward(6, 10)
 
     @pl.loop(0, nz)
     def _(k):
-        from_col = 2 * ((z + nz - k) % nz) + 1 - core
-        to(x_ref, gat.at[from_col], fs.at[k], fr.at[k], r, other).wait_recv()
+        to(x_ref, gat.at[k], fs.at[k], fr.at[k], r, other).wait_recv()
 
     for g in range(nx):
         xg = (x0 + g) % nx
@@ -175,14 +205,33 @@
         groups = pl.ds(ny * xg, ny)
         to(give.at[groups], take.at[groups], es.at[g], er.at[g], r, other).wait()
 
-    for k in range(nz):
-        at = (z + k) % nz
-        mine = pair[pl.ds(2 * at + core, 1)] + take[pl.ds(at, 1)].astype(F32)
-        if k == 0:
-            pair[pl.ds(c, 1)] = mine
-        else:
-            give[pl.ds(at, 1)] = mine.astype(BF16)
-            to(give.at[at], landed.at[k], qs.at[k], qr.at[k], r, z_peer(k)).start()
+    def chips_term(d):
+        at = chip(d)
+        return pair[pl.ds(2 * at + core, 1)] + take[pl.ds(at, 1)].astype(F32)
+
+    near = [(-1, 0, (0, 4, -4, 8)), (1, 4, (0, 4, -4, 8)), (-2, 8, (0, -4)), (2, 10, (0, 4))]
+    for m, (hop, at, offsets) in enumerate(near):
+        for j, of in enumerate(offsets):
+            near_out[pl.ds(at + j, 1)] = chips_term(hop + of).astype(BF16)
+        span = pl.ds(at, len(offsets))
+        to(
+            near_out.at[span], near_in.at[span], qs.at[m], qr.at[m], r, 2 * chip(hop) + core
+        ).start()
+    for m, (hop, at, offsets) in enumerate(near):
+        span = pl.ds(at, len(offsets))
+        to(near_out.at[span], near_in.at[span], qs.at[m], qr.at[m], r, other).wait_recv()
+
+    def gathered_term(d, *slots):
+        term = chips_term(d)
+        for slot in slots:
+            term = term + near_in[slot : slot + 1].astype(F32)
+        return term
+
+    for m, (d, slots) in enumerate(((8, (3, 7)), (4, (1, 5, 11)), (-4, (2, 6, 9)))):
+        far_out[m : m + 1] = gathered_term(d, *slots).astype(BF16)
+        to(
+            far_out.at[m], far_in.at[m], us.at[m], ur.at[m], r, 2 * chip(d) + core
+        ).start()
 
     wg_ref[...] = lax.dot_general(
         gat[...].reshape(rows * toks, width),
@@ -191,19 +240,25 @@
         preferred_element_type=F32,
     )
 
-    total = pair[pl.ds(c, 1)].reshape(share, width)
-    for k in range(1, nz):
-        to(give.at[k], landed.at[k], qs.at[k], qr.at[k], r, other).wait_recv()
-        total = total + landed[k].astype(F32)
-    ig_ref[...] = total.astype(BF16)
-
-    to(x_ref, gat.at[c], fs.at[0], fr.at[0], r, other).wait_send()
-
-    @pl.loop(1, nz)
+    total = gathered_term(0, 0, 4, 8, 10)
+    for m in (1, 2, 0):
+        to(far_out.at[m], far_in.at[m], us.at[m], ur.at[m], r, other).wait_recv()
+        total = total + far_in[m : m + 1].astype(F32)
+    ig_ref[...] = total.reshape(share, width).astype(BF16)
+
+    @pl.loop(0, last)
     def _(k):
         to(x_ref, gat.at[c], zs.at[k], zr.at[k], r, other).wait_send()
+
+    @pl.loop(0, last + 1)
+    def _(k):
         to(x_ref, gat.at[c], fs.at[k], fr.at[k], r, other).wait_send()
-        to(give.at[0], landed.at[k], qs.at[k], qr.at[k], r, other).wait_send()
+
+    for m, (hop, at, offsets) in enumerate(near):
+        span = pl.ds(at, len(offsets))
+        to(near_out.at[span], near_in.at[span], qs.at[m], qr.at[m], r, other).wait_send()
+    for m in range(3):
+        to(far_out.at[m], far_in.at[m], us.at[m], ur.at[m], r, other).wait_send()
 
     @pl.loop(1, rows)
     def _(k):
@@ -235,7 +290,10 @@
             pltpu.VMEM((nz, share, width), BF16),
             pltpu.VMEM((nz, share, width), BF16),
             pltpu.VMEM((cols, share, width), F32),
-            pltpu.VMEM((nz, share, width), BF16),
+            pltpu.VMEM((12, share, width), BF16),
+            pltpu.VMEM((12, share, width), BF16),
+            pltpu.VMEM((3, share, width), BF16),
+            pltpu.VMEM((3, share, width), BF16),
             pltpu.VMEM((toks, hidden), F32),
             dma((nz,)),
             dma((nz,)),
@@ -247,11 +305,13 @@
             dma((rows,)),
             dma((ny,)),
             dma((ny,)),
-            dma((nz,)),
-            dma((nz,)),
+            dma((4,)),
+            dma((4,)),
+            dma((3,)),
+            dma((3,)),
         ],
         compiler_params=pltpu.CompilerParams(
-            collective_id=0, has_side_effects=True, vmem_limit_bytes=56 * 1024 * 1024
+            collective_id=0, has_side_effects=True, vmem_limit_bytes=24 * 1024 * 1024
         ),
     )(inputs, weight, cotangent)
 

time: 98.8 us -> 87.8 us (0.89)
  the two profiles are of different devices: /device:TPU:1 before, /device:TPU:61 now
where the time goes in v2:
time: 87.8 us; the launch traced here: 87.5 us
  Pallas kernels  82.6 us (94%)
  local copies, waits for them, and re-layouts  4.28 us (5%)
    pallas_call x1, Pallas kernels, shards(): pl.pallas_call(functools.partial(kernel, rows, cols), out_shape=(jax.Shap...  82.6 us
    unnamed x8, local copies, waits for them, and re-layouts  4.28 us

profile of v2, /device:TPU:61, one launch (start us, length us, event | category | flops | bytes accessed | tf_op | source)
XLA Modules:
  0.0 87.5 jit_solution(13603163080222047006)
XLA Ops:
  0.6 0.0 copy-start
  0.6 1.1 %copy-done = bf16[384,768]{1,0:T(8,128)(2,1)S(1)} copy-done((bf16[384,768]{1,0:T(8,128)(2,1)S(1)}, bf16[384,768]{1,0:T(8,128)(2,1)}, u32[]{:S(2)}) %copy-start) | copy-done | bytes 589848
  1.7 0.0 copy-start.1
  1.7 0.9 %copy-done.1 = bf16[48,768]{1,0:T(8,128)(2,1)S(1)} copy-done((bf16[48,768]{1,0:T(8,128)(2,1)S(1)}, bf16[48,768]{1,0:T(8,128)(2,1)}, u32[]{:S(2)}) %copy-start.1) | copy-done | bytes 73752
  2.6 0.0 copy-start.2
  2.6 0.7 copy-done.2
  3.3 82.6 %shard_map.50 = (bf16[24,384]{1,0:T(8,128)(2,1)S(1)}, f32[384,768]{1,0:T(8,128)S(1)}) custom-call(bf16[24,384]{1,0:T(8,128)(2,1)S(1)} %copy-done.2, bf16[384,768]{1,0:T(8,128)(2,1)S(1)} %copy-done, bf16[48,768]{1,0:T(8,128)(2,1)S(1)} %copy-done.1), custom_call_target="tpu_custom_call" | custom-call | tf_op jit(solution)/shard_map/pallas_call | solution.py:276
  85.9 0.6 copy.7
  86.5 1.0 %copy.8 = f32[384,768]{1,0:T(8,128)} copy(f32[384,768]{1,0:T(8,128)S(1)} %get-tuple-element.5) | data formatting | bytes 2359296
Async XLA Ops:
  0.6 1.1 %copy-start = (bf16[384,768]{1,0:T(8,128)(2,1)S(1)}, bf16[384,768]{1,0:T(8,128)(2,1)}, u32[]{:S(2)}) copy-start(bf16[384,768]{1,0:T(8,128)(2,1)} %w_ref.1) | copy-start | bytes 1769476
  1.7 0.9 %copy-start.1 = (bf16[48,768]{1,0:T(8,128)(2,1)S(1)}, bf16[48,768]{1,0:T(8,128)(2,1)}, u32[]{:S(2)}) copy-start(bf16[48,768]{1,0:T(8,128)(2,1)} %ct_ref.1) | copy-start | bytes 221188
  2.6 0.7 copy-start.2

commit v3 on v2

--- a/solution.py
+++ b/solution.py
@@ -24,15 +24,19 @@
     rows,
     cols,
     x_ref,
+    w_hbm,
+    ct_hbm,
+    ig_ref,
+    wg_ref,
     w_ref,
     ct_ref,
-    ig_ref,
-    wg_ref,
     gat,
-    part,
-    pin,
+    out1,
+    in1,
+    kept,
+    out2,
+    in2,
     gh,
-    full,
     give,
     take,
     pair,
@@ -40,13 +44,13 @@
     near_in,
     far_out,
     far_in,
-    acc,
+    load,
     zs,
     zr,
     fs,
     fr,
-    ps,
-    pr,
+    ss,
+    sr,
     gs,
     gr,
     es,
@@ -56,29 +60,38 @@
     us,
     ur,
 ):
-    ny = math.isqrt(rows)
-    nx = rows // ny
+    n = math.isqrt(rows)
     nz = cols // 2
     r = lax.axis_index("row")
     c = lax.axis_index("col")
     z = c // 2
     core = c % 2
     other = 2 * z + 1 - core
-    x0 = r // ny
-    y0 = r % ny
+    here = (r // n, r % n)
     share = x_ref.shape[0]
     width = x_ref.shape[1]
-    hidden = w_ref.shape[1]
-    toks = ct_ref.shape[0]
+    hidden = w_hbm.shape[1]
+    half = hidden // 2
+    toks = ct_hbm.shape[0]
+    sides = (pl.ds(0, half), pl.ds(half, half))
+
+    weight_load = pltpu.make_async_copy(w_hbm, w_ref, load.at[0])
+    cotangent_load = pltpu.make_async_copy(ct_hbm, ct_ref, load.at[1])
+    own_load = pltpu.make_async_copy(x_ref, gat.at[c], load.at[2])
+    weight_load.start()
+    cotangent_load.start()
+    own_load.start()
 
     def chip(d):
         return (z + d + 2 * nz) % nz
 
-    def row_at(k):
-        return ((x0 + k // ny) % nx) * ny + (y0 + k % ny) % ny
-
-    def row_from(k):
-        return ((x0 + nx - k // ny) % nx) * ny + (y0 + ny - k % ny) % ny
+    def along(axis, d):
+        return (here[axis] + n + d) % n
+
+    def row_peer(axis, d):
+        if axis == 0:
+            return along(0, d) * n + here[1]
+        return here[0] * n + along(1, d)
 
     def to(src, dst, send, recv, row, col):
         return pltpu.make_async_remote_copy(
@@ -97,12 +110,14 @@
             barrier, inc=1, device_id=(r, 2 * chip(d) + core), device_id_type=MESH
         )
 
-    @pl.loop(1, rows)
-    def _(k):
-        pl.semaphore_signal(barrier, inc=1, device_id=(row_at(k), c), device_id_type=MESH)
+    for axis in (0, 1):
+        for d in range(1, n):
+            pl.semaphore_signal(
+                barrier, inc=1, device_id=(row_peer(axis, d), c), device_id_type=MESH
+            )
 
     pl.semaphore_signal(barrier, inc=1, device_id=(r, other), device_id_type=MESH)
-    pl.semaphore_wait(barrier, 6 + rows - 1 + 1)
+    pl.semaphore_wait(barrier, 6 + 2 * (n - 1) + 1)
 
     turn = 1 - 2 * core
     messages = [(-4, 0), (4, 0), (-4 * turn, 4 * turn)]
@@ -131,7 +146,6 @@
     last = len(messages)
     gather_send(0, 1, 3, 7, 11, 13)
     to(x_ref, gat.at[c], fs.at[last], fr.at[last], r, other).start()
-    gat[pl.ds(c, 1)] = x_ref[...].reshape(1, share, width)
     gather_wait(3, 7)
     forward(3, 7)
     gather_wait(11, 13)
@@ -153,56 +167,96 @@
     def _(k):
         to(x_ref, gat.at[k], fs.at[k], fr.at[k], r, other).wait_recv()
 
-    for g in range(nx):
-        xg = (x0 + g) % nx
-        lhs = gat[pl.ds(2 * ny * xg, 2 * ny)].reshape(ny * toks, width)
-        block = jnp.dot(lhs, w_ref[...], preferred_element_type=F32)
-        if g == 0:
-            full[...] = block.reshape(ny, toks, hidden)
-            acc[...] = full[pl.ds(y0, 1)].reshape(toks, hidden)
-        part[pl.ds(ny * xg, ny)] = block.astype(BF16).reshape(ny, toks, hidden)
-
-        @pl.loop(1 if g == 0 else 0, ny)
-        def _(j):
-            k = g * ny + j
-            peer = row_at(k)
-            to(part.at[peer], pin.at[k], ps.at[k], pr.at[k], peer, c).start()
-
-    @pl.loop(1, rows)
-    def _(k):
-        to(part.at[k], pin.at[k], ps.at[k], pr.at[k], r, other).wait_recv()
-        acc[...] += pin[pl.ds(k, 1)].reshape(toks, hidden).astype(F32)
-
-    gh[pl.ds(r, 1)] = (
-        (ct_ref[...].astype(F32) * gelu_slope(acc[...])).astype(BF16).reshape(1, toks, hidden)
-    )
-
-    @pl.loop(1, rows)
-    def _(k):
-        to(gh.at[r], gh.at[r], gs.at[k], gr.at[k], row_at(k), c).start()
-
-    for g in range(nx):
-        xg = (x0 + nx - g) % nx
-
-        @pl.loop(1 if g == 0 else 0, ny)
-        def _(j):
-            k = g * ny + j
-            to(gh.at[r], gh.at[row_from(k)], gs.at[k], gr.at[k], r, other).wait_recv()
-
-        lhs = gh[pl.ds(ny * xg, ny)].reshape(ny * toks, hidden)
+    own_load.wait()
+    weight_load.wait()
+
+    def tokens_at(axis, at):
+        if axis == 0:
+            picked = gat[pl.ds(2 * n * at, 2 * n)]
+        else:
+            picked = jnp.concatenate([gat[pl.ds(2 * (n * v + at), 2)] for v in range(n)], axis=0)
+        return picked.reshape(n * toks, width)
+
+    far_first = (2, 1, 3)
+    for d in far_first + (0,):
+        for h in (0, 1):
+            term = jnp.dot(
+                tokens_at(h, along(h, d)), w_ref[:, sides[h]], preferred_element_type=F32
+            )
+            if d == 0:
+                kept[h] = term.reshape(n, toks, half)
+            else:
+                out1[h, d] = term.astype(BF16).reshape(n, toks, half)
+                to(
+                    out1.at[h, d], in1.at[h, d], ss.at[0, h, d], sr.at[0, h, d], row_peer(h, d), c
+                ).start()
+
+    for h in (0, 1):
+        for d in (1, 3, 2):
+            to(out1.at[h, d], in1.at[h, d], ss.at[0, h, d], sr.at[0, h, d], r, other).wait_recv()
+        kept[h] += in1[h, 1].astype(F32) + in1[h, 2].astype(F32) + in1[h, 3].astype(F32)
+        for d in far_first:
+            at = along(1 - h, d)
+            out2[h, d] = kept[h, pl.ds(at, 1)].reshape(toks, half).astype(BF16)
+            to(
+                out2.at[h, d], in2.at[h, d], ss.at[1, h, d], sr.at[1, h, d], row_peer(1 - h, d), c
+            ).start()
+
+    cotangent_load.wait()
+    for h in (0, 1):
+        preact = kept[h, pl.ds(here[1 - h], 1)].reshape(toks, half)
+        for d in (1, 3, 2):
+            to(out2.at[h, d], in2.at[h, d], ss.at[1, h, d], sr.at[1, h, d], r, other).wait_recv()
+            preact = preact + in2[h, d].astype(F32)
+        grad = (ct_ref[:, sides[h]].astype(F32) * gelu_slope(preact)).astype(BF16)
+        gh[h, pl.ds(here[1 - h], 1), pl.ds(here[h], 1)] = grad.reshape(1, 1, toks, half)
+        own = gh.at[h, here[1 - h], here[h]]
+        for d in far_first:
+            to(own, own, gs.at[h, 0, d], gr.at[h, 0, d], row_peer(h, d), c).start()
+        for d in far_first:
+            to(own, own, gs.at[h, 1, d], gr.at[h, 1, d], row_peer(1 - h, d), c).start()
+
+    for e in (1, 3, 2):
+        for h in (0, 1):
+            block = gh.at[h, here[1 - h], along(h, -e)]
+            to(block, block, gs.at[h, 0, e], gr.at[h, 0, e], r, other).wait_recv()
+            for d in far_first:
+                to(
+                    block, block, gs.at[h, 1 + e, d], gr.at[h, 1 + e, d], row_peer(1 - h, d), c
+                ).start()
+
+    def second_wait(h, e, d):
+        block = gh.at[h, along(1 - h, -d), along(h, -e)]
+        to(block, block, gs.at[h, 1 + e, d], gr.at[h, 1 + e, d], r, other).wait_recv()
+
+    for g, e in enumerate((0, 1, 3, 2)):
+        xg = along(0, -e)
+        for d in (1, 3, 2):
+            second_wait(0, e, d)
+        if e > 0:
+            for f in (0, 1, 3, 2):
+                second_wait(1, f, e)
+        lhs = jnp.concatenate([gh[0, v, pl.ds(xg, 1)] for v in range(n)], axis=0)
         block = lax.dot_general(
-            lhs, w_ref[...], (((1,), (1,)), ((), ())), preferred_element_type=F32
+            lhs.reshape(n * toks, half),
+            w_ref[:, sides[0]],
+            (((1,), (1,)), ((), ())),
+            preferred_element_type=F32,
+        ) + lax.dot_general(
+            gh[1, pl.ds(xg, 1)].reshape(n * toks, half),
+            w_ref[:, sides[1]],
+            (((1,), (1,)), ((), ())),
+            preferred_element_type=F32,
         )
-        pair[pl.ds(2 * ny * xg, 2 * ny)] = block.reshape(2 * ny, share, width)
-        for j in range(ny):
-            at = ny * xg + j
+        pair[pl.ds(2 * n * xg, 2 * n)] = block.reshape(2 * n, share, width)
+        for j in range(n):
+            at = n * xg + j
             give[pl.ds(at, 1)] = pair[pl.ds(2 * at + 1 - core, 1)].astype(BF16)
-        groups = pl.ds(ny * xg, ny)
+        groups = pl.ds(n * xg, n)
         to(give.at[groups], take.at[groups], es.at[g], er.at[g], r, other).start()
 
-    for g in range(nx):
-        xg = (x0 + nx - g) % nx
-        groups = pl.ds(ny * xg, ny)
+    for g, e in enumerate((0, 1, 3, 2)):
+        groups = pl.ds(n * along(0, -e), n)
         to(give.at[groups], take.at[groups], es.at[g], er.at[g], r, other).wait()
 
     def chips_term(d):
@@ -233,12 +287,16 @@
             far_out.at[m], far_in.at[m], us.at[m], ur.at[m], r, 2 * chip(d) + core
         ).start()
 
-    wg_ref[...] = lax.dot_general(
-        gat[...].reshape(rows * toks, width),
-        gh[...].reshape(rows * toks, hidden),
-        (((0,), (0,)), ((), ())),
-        preferred_element_type=F32,
+    by_column = jnp.concatenate(
+        [gat[2 * (n * u + v) : 2 * (n * u + v) + 2] for v in range(n) for u in range(n)], axis=0
     )
+    for h, tokens in ((0, by_column), (1, gat[...])):
+        wg_ref[:, sides[h]] = lax.dot_general(
+            tokens.reshape(rows * toks, width),
+            gh[h].reshape(rows * toks, half),
+            (((0,), (0,)), ((), ())),
+            preferred_element_type=F32,
+        )
 
     total = gathered_term(0, 0, 4, 8, 10)
     for m in (1, 2, 0):
@@ -260,10 +318,15 @@
     for m in range(3):
         to(far_out.at[m], far_in.at[m], us.at[m], ur.at[m], r, other).wait_send()
 
-    @pl.loop(1, rows)
-    def _(k):
-        to(part.at[k], pin.at[k], ps.at[k], pr.at[k], r, other).wait_send()
-        to(gh.at[r], gh.at[r], gs.at[k], gr.at[k], r, other).wait_send()
+    for h in (0, 1):
+
+        @pl.loop(1, n)
+        def _(d):
+            to(out1.at[h, d], in1.at[h, d], ss.at[0, h, d], sr.at[0, h, d], r, other).wait_send()
+            to(out2.at[h, d], in2.at[h, d], ss.at[1, h, d], sr.at[1, h, d], r, other).wait_send()
+            for e in range(n + 1):
+                block = gh.at[h, 0, 0]
+                to(block, block, gs.at[h, e, d], gr.at[h, e, d], r, other).wait_send()
 
 
 def shards(rows, cols, inputs, weight, cotangent):
@@ -271,7 +334,8 @@
     hidden = weight.shape[1]
     toks = cotangent.shape[0]
     nz = cols // 2
-    ny = math.isqrt(rows)
+    n = math.isqrt(rows)
+    half = hidden // 2
     dma = pltpu.SemaphoreType.DMA
     return pl.pallas_call(
         functools.partial(kernel, rows, cols),
@@ -279,14 +343,18 @@
             jax.ShapeDtypeStruct((share, width), BF16),
             jax.ShapeDtypeStruct((width, hidden), F32),
         ),
-        in_specs=[pl.BlockSpec(memory_space=pltpu.VMEM)] * 3,
+        in_specs=[pl.BlockSpec(memory_space=pltpu.HBM)] * 3,
         out_specs=(pl.BlockSpec(memory_space=pltpu.VMEM),) * 2,
         scratch_shapes=[
+            pltpu.VMEM((width, hidden), BF16),
+            pltpu.VMEM((toks, hidden), BF16),
             pltpu.VMEM((cols, share, width), BF16),
-            pltpu.VMEM((rows, toks, hidden), BF16),
-            pltpu.VMEM((rows, toks, hidden), BF16),
-            pltpu.VMEM((rows, toks, hidden), BF16),
-            pltpu.VMEM((ny, toks, hidden), F32),
+            pltpu.VMEM((2, n, n, toks, half), BF16),
+            pltpu.VMEM((2, n, n, toks, half), BF16),
+            pltpu.VMEM((2, n, toks, half), F32),
+            pltpu.VMEM((2, n, toks, half), BF16),
+            pltpu.VMEM((2, n, toks, half), BF16),
+            pltpu.VMEM((2, n, n, toks, half), BF16),
             pltpu.VMEM((nz, share, width), BF16),
             pltpu.VMEM((nz, share, width), BF16),
             pltpu.VMEM((cols, share, width), F32),
@@ -294,17 +362,17 @@
             pltpu.VMEM((12, share, width), BF16),
             pltpu.VMEM((3, share, width), BF16),
             pltpu.VMEM((3, share, width), BF16),
-            pltpu.VMEM((toks, hidden), F32),
+            dma((3,)),
             dma((nz,)),
             dma((nz,)),
             dma((nz,)),
             dma((nz,)),
-            dma((rows,)),
-            dma((rows,)),
-            dma((rows,)),
-            dma((rows,)),
-            dma((ny,)),
-            dma((ny,)),
+            dma((2, 2, n)),
+            dma((2, 2, n)),
+            dma((2, n + 1, n)),
+            dma((2, n + 1, n)),
+            dma((n,)),
+            dma((n,)),
             dma((4,)),
             dma((4,)),
             dma((3,)),

time: 87.8 us -> 76.3 us (0.87)
  the two profiles are of different devices: /device:TPU:61 before, /device:TPU:32 now
where the time goes in v3:
time: 76.3 us; the launch traced here: 76 us
  Pallas kernels  71.1 us (93%)
  local copies, waits for them, and re-layouts  4.28 us (6%)
    pallas_call x1, Pallas kernels, shards(): pl.pallas_call(functools.partial(kernel, rows, cols), out_shape=(jax.Shap...  71.1 us
    unnamed x8, local copies, waits for them, and re-layouts  4.28 us

profile of v3, /device:TPU:32, one launch (start us, length us, event | category | flops | bytes accessed | tf_op | source)
XLA Modules:
  0.0 76.0 jit_solution(15324340594132237508)
XLA Ops:
  0.6 0.0 copy-start
  0.6 1.1 %copy-done = bf16[384,768]{1,0:T(8,128)(2,1)S(1)} copy-done((bf16[384,768]{1,0:T(8,128)(2,1)S(1)}, bf16[384,768]{1,0:T(8,128)(2,1)}, u32[]{:S(2)}) %copy-start) | copy-done | bytes 589848
  1.7 0.0 copy-start.1
  1.7 0.9 %copy-done.1 = bf16[48,768]{1,0:T(8,128)(2,1)S(1)} copy-done((bf16[48,768]{1,0:T(8,128)(2,1)S(1)}, bf16[48,768]{1,0:T(8,128)(2,1)}, u32[]{:S(2)}) %copy-start.1) | copy-done | bytes 73752
  2.6 0.0 copy-start.2
  2.6 0.7 copy-done.2
  3.3 71.1 %shard_map.50 = (bf16[24,384]{1,0:T(8,128)(2,1)S(1)}, f32[384,768]{1,0:T(8,128)S(1)}) custom-call(bf16[24,384]{1,0:T(8,128)(2,1)S(1)} %copy-done.2, bf16[384,768]{1,0:T(8,128)(2,1)S(1)} %copy-done, bf16[48,768]{1,0:T(8,128)(2,1)S(1)} %copy-done.1), custom_call_target="tpu_custom_call" | custom-call | tf_op jit(solution)/shard_map/pallas_call | solution.py:340
  74.4 0.6 copy.7
  75.0 1.0 %copy.8 = f32[384,768]{1,0:T(8,128)} copy(f32[384,768]{1,0:T(8,128)S(1)} %get-tuple-element.5) | data formatting | bytes 2359296
Async XLA Ops:
  0.6 1.1 %copy-start = (bf16[384,768]{1,0:T(8,128)(2,1)S(1)}, bf16[384,768]{1,0:T(8,128)(2,1)}, u32[]{:S(2)}) copy-start(bf16[384,768]{1,0:T(8,128)(2,1)} %w_hbm.1) | copy-start | bytes 1769476
  1.7 0.9 %copy-start.1 = (bf16[48,768]{1,0:T(8,128)(2,1)S(1)}, bf16[48,768]{1,0:T(8,128)(2,1)}, u32[]{:S(2)}) copy-start(bf16[48,768]{1,0:T(8,128)(2,1)} %ct_hbm.1) | copy-start | bytes 221188
  2.6 0.7 copy-start.2

commit v4 on v3

--- a/solution.py
+++ b/solution.py
@@ -213,14 +213,14 @@
         own = gh.at[h, here[1 - h], here[h]]
         for d in far_first:
             to(own, own, gs.at[h, 0, d], gr.at[h, 0, d], row_peer(h, d), c).start()
-        for d in far_first:
+        for d in (1, 3):
             to(own, own, gs.at[h, 1, d], gr.at[h, 1, d], row_peer(1 - h, d), c).start()
 
     for e in (1, 3, 2):
         for h in (0, 1):
             block = gh.at[h, here[1 - h], along(h, -e)]
             to(block, block, gs.at[h, 0, e], gr.at[h, 0, e], r, other).wait_recv()
-            for d in far_first:
+            for d in (1, 3):
                 to(
                     block, block, gs.at[h, 1 + e, d], gr.at[h, 1 + e, d], row_peer(1 - h, d), c
                 ).start()
@@ -229,13 +229,27 @@
         block = gh.at[h, along(1 - h, -d), along(h, -e)]
         to(block, block, gs.at[h, 1 + e, d], gr.at[h, 1 + e, d], r, other).wait_recv()
 
+    def pass_on(e):
+        for h in (0, 1):
+            for d in (1, 3):
+                second_wait(h, e, d)
+                if (d == 1) == (e < 2):
+                    block = gh.at[h, along(1 - h, -d), along(h, -e)]
+                    to(
+                        block, block, gs.at[h, 1 + e, 2], gr.at[h, 1 + e, 2], row_peer(1 - h, d), c
+                    ).start()
+
+    pass_on(0)
+    pass_on(1)
+    pass_on(3)
     for g, e in enumerate((0, 1, 3, 2)):
+        if g == 1:
+            pass_on(2)
         xg = along(0, -e)
-        for d in (1, 3, 2):
-            second_wait(0, e, d)
-        if e > 0:
+        second_wait(0, e, 2)
+        if e == 2:
             for f in (0, 1, 3, 2):
-                second_wait(1, f, e)
+                second_wait(1, f, 2)
         lhs = jnp.concatenate([gh[0, v, pl.ds(xg, 1)] for v in range(n)], axis=0)
         block = lax.dot_general(
             lhs.reshape(n * toks, half),
@@ -381,7 +395,7 @@
         compiler_params=pltpu.CompilerParams(
             collective_id=0, has_side_effects=True, vmem_limit_bytes=24 * 1024 * 1024
         ),
-    )(inputs, weight, cotangent)
+    )(*(pltpu.with_memory_space_constraint(a, pltpu.HBM) for a in (inputs, weight, cotangent)))
 
 
 def solution(mesh):

time: 76.3 us -> 73.1 us (0.958)
  the two profiles are of different devices: /device:TPU:32 before, /device:TPU:6 now
where the time goes in v4:
time: 73.1 us; the launch traced here: 72.6 us
  Pallas kernels  70.3 us (96%)
  local copies, waits for them, and re-layouts  1.62 us (2%)
    pallas_call x1, Pallas kernels, shards(): pl.pallas_call(functools.partial(kernel, rows, cols), out_shape=(jax.Shap...  70.3 us
    unnamed x2, local copies, waits for them, and re-layouts  1.62 us

profile of v4, /device:TPU:6, one launch (start us, length us, event | category | flops | bytes accessed | tf_op | source)
XLA Modules:
  0.0 72.6 jit_solution(17339513446558467993)
XLA Ops:
  0.6 70.3 %shard_map.50 = (bf16[24,384]{1,0:T(8,128)(2,1)S(1)}, f32[384,768]{1,0:T(8,128)S(1)}) custom-call(bf16[24,384]{1,0:T(8,128)(2,1)} %x_ref.1, bf16[384,768]{1,0:T(8,128)(2,1)} %w_hbm.1, bf16[48,768]{1,0:T(8,128)(2,1)} %ct_hbm.1), custom_call_target="tpu_custom_call" | custom-call | tf_op jit(solution)/shard_map/pallas_call | solution.py:354
  71.0 0.6 copy.7
  71.6 1.0 %copy.8 = f32[384,768]{1,0:T(8,128)} copy(f32[384,768]{1,0:T(8,128)S(1)} %get-tuple-element.5) | data formatting | bytes 2359296

commit v5 on v4

--- a/solution.py
+++ b/solution.py
@@ -105,7 +105,7 @@
 
     barrier = pltpu.get_barrier_semaphore()
 
-    for d in (-4, 4, -2, 2, -1, 1):
+    for d in (-4, 4, -3, 3, -2, 2, -1, 1):
         pl.semaphore_signal(
             barrier, inc=1, device_id=(r, 2 * chip(d) + core), device_id_type=MESH
         )
@@ -117,11 +117,11 @@
             )
 
     pl.semaphore_signal(barrier, inc=1, device_id=(r, other), device_id_type=MESH)
-    pl.semaphore_wait(barrier, 6 + 2 * (n - 1) + 1)
+    pl.semaphore_wait(barrier, 8 + 2 * (n - 1) + 1)
 
     turn = 1 - 2 * core
     messages = [(-4, 0), (4, 0), (-4 * turn, 4 * turn)]
-    messages += [(-1, of) for of in (0, 4, -4, 8)] + [(1, of) for of in (0, 4, -4, 8)]
+    messages += [(-1, 0), (-1, 4), (-1, -4), (-3, 4), (1, 0), (1, 4), (1, -4), (3, -4)]
     messages += [(-2, 0), (-2, 4), (2, 0), (2, -4)]
 
     def gather_send(*numbers):
@@ -151,17 +151,16 @@
     gather_wait(11, 13)
     forward(11, 13)
     gather_wait(0, 1)
-    gather_send(2, 4, 8, 5, 9, 12, 14)
+    gather_send(2, 6, 10, 4, 8, 5, 9, 12, 14)
     forward(0, 1)
     gather_wait(4, 5, 8, 9)
     forward(4, 5, 8, 9)
-    gather_wait(2)
-    gather_send(6, 10)
-    forward(2)
     gather_wait(12, 14)
     forward(12, 14)
     gather_wait(6, 10)
     forward(6, 10)
+    gather_wait(2)
+    forward(2)
 
     @pl.loop(0, nz)
     def _(k):
@@ -277,26 +276,25 @@
         at = chip(d)
         return pair[pl.ds(2 * at + core, 1)] + take[pl.ds(at, 1)].astype(F32)
 
-    near = [(-1, 0, (0, 4, -4, 8)), (1, 4, (0, 4, -4, 8)), (-2, 8, (0, -4)), (2, 10, (0, 4))]
-    for m, (hop, at, offsets) in enumerate(near):
-        for j, of in enumerate(offsets):
-            near_out[pl.ds(at + j, 1)] = chips_term(hop + of).astype(BF16)
-        span = pl.ds(at, len(offsets))
-        to(
-            near_out.at[span], near_in.at[span], qs.at[m], qr.at[m], r, 2 * chip(hop) + core
-        ).start()
-    for m, (hop, at, offsets) in enumerate(near):
-        span = pl.ds(at, len(offsets))
-        to(near_out.at[span], near_in.at[span], qs.at[m], qr.at[m], r, other).wait_recv()
-
-    def gathered_term(d, *slots):
-        term = chips_term(d)
-        for slot in slots:
+    steps = (1, -1, 2, -2, 3, -3)
+    near = [(4 * turn, 8)] + [(d, d + 4 if d > 0 else d - 4) for d in reversed(steps)]
+    near += [(d, d) for d in reversed(steps)]
+
+    def near_copy(m, col):
+        return to(near_out.at[m], near_in.at[m], qs.at[m], qr.at[m], r, col)
+
+    for m, (hop, keeper) in enumerate(near):
+        near_out[m : m + 1] = chips_term(keeper).astype(BF16)
+        near_copy(m, 2 * chip(hop) + core).start()
+    for m in range(7):
+        near_copy(m, other).wait_recv()
+
+    opposite = near_in[0:1].astype(F32)
+    for m, d in enumerate((4, -4)):
+        term = chips_term(d) + jnp.where(core == m, opposite, 0.0)
+        for slot in (2 - m, 4 - m, 6 - m):
             term = term + near_in[slot : slot + 1].astype(F32)
-        return term
-
-    for m, (d, slots) in enumerate(((8, (3, 7)), (4, (1, 5, 11)), (-4, (2, 6, 9)))):
-        far_out[m : m + 1] = gathered_term(d, *slots).astype(BF16)
+        far_out[m : m + 1] = term.astype(BF16)
         to(
             far_out.at[m], far_in.at[m], us.at[m], ur.at[m], r, 2 * chip(d) + core
         ).start()
@@ -312,8 +310,11 @@
             preferred_element_type=F32,
         )
 
-    total = gathered_term(0, 0, 4, 8, 10)
-    for m in (1, 2, 0):
+    total = chips_term(0)
+    for m in range(7, 13):
+        near_copy(m, other).wait_recv()
+        total = total + near_in[m : m + 1].astype(F32)
+    for m in range(2):
         to(far_out.at[m], far_in.at[m], us.at[m], ur.at[m], r, other).wait_recv()
         total = total + far_in[m : m + 1].astype(F32)
     ig_ref[...] = total.reshape(share, width).astype(BF16)
@@ -326,10 +327,9 @@
     def _(k):
         to(x_ref, gat.at[c], fs.at[k], fr.at[k], r, other).wait_send()
 
-    for m, (hop, at, offsets) in enumerate(near):
-        span = pl.ds(at, len(offsets))
-        to(near_out.at[span], near_in.at[span], qs.at[m], qr.at[m], r, other).wait_send()
-    for m in range(3):
+    for m in range(13):
+        near_copy(m, other).wait_send()
+    for m in range(2):
         to(far_out.at[m], far_in.at[m], us.at[m], ur.at[m], r, other).wait_send()
 
     for h in (0, 1):
@@ -372,10 +372,10 @@
             pltpu.VMEM((nz, share, width), BF16),
             pltpu.VMEM((nz, share, width), BF16),
             pltpu.VMEM((cols, share, width), F32),
-            pltpu.VMEM((12, share, width), BF16),
-            pltpu.VMEM((12, share, width), BF16),
-            pltpu.VMEM((3, share, width), BF16),
-            pltpu.VMEM((3, share, width), BF16),
+            pltpu.VMEM((13, share, width), BF16),
+            pltpu.VMEM((13, share, width), BF16),
+            pltpu.VMEM((2, share, width), BF16),
+            pltpu.VMEM((2, share, width), BF16),
             dma((3,)),
             dma((nz,)),
             dma((nz,)),
@@ -387,10 +387,10 @@
             dma((2, n + 1, n)),
             dma((n,)),
             dma((n,)),
-            dma((4,)),
-            dma((4,)),
-            dma((3,)),
-            dma((3,)),
+            dma((13,)),
+            dma((13,)),
+            dma((2,)),
+            dma((2,)),
         ],
         compiler_params=pltpu.CompilerParams(
             collective_id=0, has_side_effects=True, vmem_limit_bytes=24 * 1024 * 1024

time: 73.1 us -> 69 us (0.944)
  Pallas kernels: 70.3 us -> 66.6 us
    pallas_call x1, Pallas kernels: 70.3 us -> 66.6 us  [shards(): pl.pallas_call(functools.partial(kernel, rows, cols), out_shape=(jax.Shap...]
where the time goes in v5:
time: 69 us; the launch traced here: 68.9 us
  Pallas kernels  66.6 us (97%)
  local copies, waits for them, and re-layouts  1.62 us (2%)
    pallas_call x1, Pallas kernels, shards(): pl.pallas_call(functools.partial(kernel, rows, cols), out_shape=(jax.Shap...  66.6 us
    unnamed x2, local copies, waits for them, and re-layouts  1.62 us

profile of v5, /device:TPU:6, one launch (start us, length us, event | category | flops | bytes accessed | tf_op | source)
XLA Modules:
  0.0 68.9 jit_solution(587616905992529453)
XLA Ops:
  0.6 66.6 %shard_map.50 = (bf16[24,384]{1,0:T(8,128)(2,1)S(1)}, f32[384,768]{1,0:T(8,128)S(1)}) custom-call(bf16[24,384]{1,0:T(8,128)(2,1)} %x_ref.1, bf16[384,768]{1,0:T(8,128)(2,1)} %w_hbm.1, bf16[48,768]{1,0:T(8,128)(2,1)} %ct_hbm.1), custom_call_target="tpu_custom_call" | custom-call | tf_op jit(solution)/shard_map/pallas_call | solution.py:354
  67.2 0.6 copy.7
  67.9 1.0 %copy.8 = f32[384,768]{1,0:T(8,128)} copy(f32[384,768]{1,0:T(8,128)S(1)} %get-tuple-element.5) | data formatting | bytes 2359296

commit v6 on v5

--- a/solution.py
+++ b/solution.py
@@ -169,41 +169,59 @@
     own_load.wait()
     weight_load.wait()
 
-    def tokens_at(axis, at):
-        if axis == 0:
-            picked = gat[pl.ds(2 * n * at, 2 * n)]
-        else:
-            picked = jnp.concatenate([gat[pl.ds(2 * (n * v + at), 2)] for v in range(n)], axis=0)
-        return picked.reshape(n * toks, width)
+    def tokens_at(axis, d):
+        at = along(axis, d)
+        picked = []
+        for off in (1, 2, 3, 0):
+            line = along(1 - axis, off)
+            block = n * at + line if axis == 0 else n * line + at
+            picked.append(gat[pl.ds(2 * block, 2)])
+        return jnp.concatenate(picked, axis=0).reshape(n * toks, width)
+
+    def passed(h, d, col):
+        span = pl.ds(0, n - 1)
+        return to(
+            out1.at[h, d, span], in1.at[h, d, span], ss.at[0, h, d], sr.at[0, h, d],
+            row_peer(h, d), col,
+        )
+
+    def stays(h, d, col):
+        return to(
+            out1.at[h, d, n - 1], in1.at[h, d, n - 1], ss.at[2, h, d], sr.at[2, h, d],
+            row_peer(h, d), col,
+        )
 
     far_first = (2, 1, 3)
     for d in far_first + (0,):
         for h in (0, 1):
-            term = jnp.dot(
-                tokens_at(h, along(h, d)), w_ref[:, sides[h]], preferred_element_type=F32
-            )
+            term = jnp.dot(tokens_at(h, d), w_ref[:, sides[h]], preferred_element_type=F32)
             if d == 0:
                 kept[h] = term.reshape(n, toks, half)
             else:
                 out1[h, d] = term.astype(BF16).reshape(n, toks, half)
-                to(
-                    out1.at[h, d], in1.at[h, d], ss.at[0, h, d], sr.at[0, h, d], row_peer(h, d), c
-                ).start()
+                passed(h, d, c).start()
+    for d in far_first:
+        for h in (0, 1):
+            stays(h, d, c).start()
 
     for h in (0, 1):
         for d in (1, 3, 2):
-            to(out1.at[h, d], in1.at[h, d], ss.at[0, h, d], sr.at[0, h, d], r, other).wait_recv()
-        kept[h] += in1[h, 1].astype(F32) + in1[h, 2].astype(F32) + in1[h, 3].astype(F32)
+            passed(h, d, c).wait_recv()
         for d in far_first:
-            at = along(1 - h, d)
-            out2[h, d] = kept[h, pl.ds(at, 1)].reshape(toks, half).astype(BF16)
+            j = d - 1
+            term = kept[h, j] + in1[h, 1, j].astype(F32)
+            term = term + in1[h, 2, j].astype(F32) + in1[h, 3, j].astype(F32)
+            out2[h, d] = term.astype(BF16)
             to(
                 out2.at[h, d], in2.at[h, d], ss.at[1, h, d], sr.at[1, h, d], row_peer(1 - h, d), c
             ).start()
 
     cotangent_load.wait()
     for h in (0, 1):
-        preact = kept[h, pl.ds(here[1 - h], 1)].reshape(toks, half)
+        preact = kept[h, n - 1]
+        for d in (1, 3, 2):
+            stays(h, d, c).wait_recv()
+            preact = preact + in1[h, d, n - 1].astype(F32)
         for d in (1, 3, 2):
             to(out2.at[h, d], in2.at[h, d], ss.at[1, h, d], sr.at[1, h, d], r, other).wait_recv()
             preact = preact + in2[h, d].astype(F32)
@@ -336,7 +354,13 @@
 
         @pl.loop(1, n)
         def _(d):
-            to(out1.at[h, d], in1.at[h, d], ss.at[0, h, d], sr.at[0, h, d], r, other).wait_send()
+            span = pl.ds(0, n - 1)
+            to(
+                out1.at[h, d, span], in1.at[h, d, span], ss.at[0, h, d], sr.at[0, h, d], r, other
+            ).wait_send()
+            to(
+                out1.at[h, d, 0], in1.at[h, d, 0], ss.at[2, h, d], sr.at[2, h, d], r, other
+            ).wait_send()
             to(out2.at[h, d], in2.at[h, d], ss.at[1, h, d], sr.at[1, h, d], r, other).wait_send()
             for e in range(n + 1):
                 block = gh.at[h, 0, 0]
@@ -381,8 +405,8 @@
             dma((nz,)),
             dma((nz,)),
             dma((nz,)),
-            dma((2, 2, n)),
-            dma((2, 2, n)),
+            dma((3, 2, n)),
+            dma((3, 2, n)),
             dma((2, n + 1, n)),
             dma((2, n + 1, n)),
             dma((n,)),

time: 69 us -> 68.4 us (level)
  no operation moved by 1% of the time
where the time goes in v6:
time: 68.4 us; the launch traced here: 68.2 us
  Pallas kernels  66 us (96%)
  local copies, waits for them, and re-layouts  1.62 us (2%)
    pallas_call x1, Pallas kernels, shards(): pl.pallas_call(functools.partial(kernel, rows, cols), out_shape=(jax.Shap...  66 us
    unnamed x2, local copies, waits for them, and re-layouts  1.62 us

profile of v6, /device:TPU:6, one launch (start us, length us, event | category | flops | bytes accessed | tf_op | source)
XLA Modules:
  0.0 68.2 jit_solution(5113803767007797619)
XLA Ops:
  0.6 66.0 %shard_map.50 = (bf16[24,384]{1,0:T(8,128)(2,1)S(1)}, f32[384,768]{1,0:T(8,128)S(1)}) custom-call(bf16[24,384]{1,0:T(8,128)(2,1)} %x_ref.1, bf16[384,768]{1,0:T(8,128)(2,1)} %w_hbm.1, bf16[48,768]{1,0:T(8,128)(2,1)} %ct_hbm.1), custom_call_target="tpu_custom_call" | custom-call | tf_op jit(solution)/shard_map/pallas_call | solution.py:378
  66.6 0.6 copy.7
  67.2 1.0 %copy.8 = f32[384,768]{1,0:T(8,128)} copy(f32[384,768]{1,0:T(8,128)S(1)} %get-tuple-element.5) | data formatting | bytes 2359296

commit v7 on v6

--- a/solution.py
+++ b/solution.py
@@ -304,6 +304,16 @@
     for m, (hop, keeper) in enumerate(near):
         near_out[m : m + 1] = chips_term(keeper).astype(BF16)
         near_copy(m, 2 * chip(hop) + core).start()
+
+    def weight_half(h, tokens):
+        wg_ref[:, sides[h]] = lax.dot_general(
+            tokens.reshape(rows * toks, width),
+            gh[h].reshape(rows * toks, half),
+            (((0,), (0,)), ((), ())),
+            preferred_element_type=F32,
+        )
+
+    weight_half(1, gat[...])
     for m in range(7):
         near_copy(m, other).wait_recv()
 
@@ -320,13 +330,7 @@
     by_column = jnp.concatenate(
         [gat[2 * (n * u + v) : 2 * (n * u + v) + 2] for v in range(n) for u in range(n)], axis=0
     )
-    for h, tokens in ((0, by_column), (1, gat[...])):
-        wg_ref[:, sides[h]] = lax.dot_general(
-            tokens.reshape(rows * toks, width),
-            gh[h].reshape(rows * toks, half),
-            (((0,), (0,)), ((), ())),
-            preferred_element_type=F32,
-        )
+    weight_half(0, by_column)
 
     total = chips_term(0)
     for m in range(7, 13):

time: 68.4 us -> 68.4 us (level)
  no operation moved by 1% of the time
where the time goes in v7:
time: 68.4 us; the launch traced here: 68.2 us
  Pallas kernels  66 us (96%)
  local copies, waits for them, and re-layouts  1.62 us (2%)
    pallas_call x1, Pallas kernels, shards(): pl.pallas_call(functools.partial(kernel, rows, cols), out_shape=(jax.Shap...  66 us
    unnamed x2, local copies, waits for them, and re-layouts  1.62 us

profile of v7, /device:TPU:6, one launch (start us, length us, event | category | flops | bytes accessed | tf_op | source)
XLA Modules:
  0.0 68.2 jit_solution(15175375725435778655)
XLA Ops:
  0.6 66.0 %shard_map.50 = (bf16[24,384]{1,0:T(8,128)(2,1)S(1)}, f32[384,768]{1,0:T(8,128)S(1)}) custom-call(bf16[24,384]{1,0:T(8,128)(2,1)} %x_ref.1, bf16[384,768]{1,0:T(8,128)(2,1)} %w_hbm.1, bf16[48,768]{1,0:T(8,128)(2,1)} %ct_hbm.1), custom_call_target="tpu_custom_call" | custom-call | tf_op jit(solution)/shard_map/pallas_call | solution.py:382
  66.6 0.6 copy.7
  67.2 1.0 %copy.8 = f32[384,768]{1,0:T(8,128)} copy(f32[384,768]{1,0:T(8,128)S(1)} %get-tuple-element.5) | data formatting | bytes 2359296
